TPU v7x, 32 devices: a whole 2x2x4 slice. The times are simulated.
32 devices in a mesh: member: 8 (over y, x, core), band: 4 (over z).
Axes of the slice: x: 2, y: 2, z: 4, core: 2. Of those that a mesh axis runs over, the one named last changes fastest.
Arguments:
- controls: float32 [16, 16, 256, 512], P('member', None, 'band'), may hold values from -6 to 6
- members: float32 [16, 16, 256, 512], P('member', None, 'band'), may hold values from -6 to 6
- loc_lon: float32 [512, 512], replicated, may hold values from -0.25 to 0.25
- loc_lat: float32 [256, 256], replicated, may hold values from -0.375 to 0.375
- balance: float32 [5, 1024, 2048], P(None, 'band', 'member'), may hold values from -1 to 1
- innovation: float32 [16, 1024, 2048], P(None, 'band', 'member'), may hold values from -6 to 6
- obs_weight: float32 [16, 1024, 2048], P(None, 'band', 'member'), may hold values from 0.2 to 5
Outputs:
- gradient: float32 [16, 16, 256, 512], P('member', None, 'band')
All inputs are finite; a program needn't handle non-finite values.
Results may differ from a plain program's by a relative error of at most 0.00012.
Values sent between devices are 32-bit elements; how exact they have to be, the bound alone decides.
No kernel may reach another device: no remote copies, remote signals or barrier semaphores. Data moves between devices by JAX's collectives and lax.ppermute only.
A program may use at most 128 MiB of HBM per device.

v0:
```python
import math
import jax
import jax.numpy as jnp
from jax import lax
from jax.sharding import PartitionSpec as P

phase_fraction = (0.625, 0.875, 0.125, 0.375)
phase_start = (0, 0, 1, 1)


def with_halo(value, sides, width, wrap):
    for axis, dim in sides:
        size, length = (lax.axis_size(axis), value.shape[dim])
        up = [(i, (i + 1) % size) for i in range(size if wrap else size - 1)]
        down = [(j, i) for i, j in up]
        last = lax.slice_in_dim(value, length - width, length, axis=dim)
        leading = lax.slice_in_dim(value, 0, width, axis=dim)
        before = lax.ppermute(last, axis, up)
        after = lax.ppermute(leading, axis, down)
        value = jnp.concatenate([before, value, after], axis=dim)
    return value


def passed_along(value, axis, by):
    length = lax.axis_size(axis)
    return lax.ppermute(value, axis, [(i, (i + by) % length) for i in range(length)])


def from_behind(value, axis, steps):
    count = lax.axis_size(axis)
    leading, last = (max(0, -steps), min(count, count - steps))
    return lax.ppermute(value, axis, [(source, source + steps) for source in range(leading, last)])


def cubic_weights(fraction):
    return (
        (-(fraction**3) + 2 * fraction**2 - fraction) / 2,
        (3 * fraction**3 - 5 * fraction**2 + 2) / 2,
        (-3 * fraction**3 + 4 * fraction**2 + fraction) / 2,
        (fraction**3 - fraction**2) / 2,
    )


def refine(padded, dim_index):
    length = padded.shape[dim_index] - 4
    phase_rows = []
    for phase_index in range(4):
        weights = cubic_weights(phase_fraction[phase_index])
        summed = jnp.zeros_like(lax.slice_in_dim(padded, 0, length, axis=dim_index))
        for tap_index in range(4):
            first = phase_start[phase_index] + tap_index
            summed = summed + weights[tap_index] * lax.slice_in_dim(
                padded, first, first + length, axis=dim_index
            )
        phase_rows.append(summed)
    stacked = jnp.stack(phase_rows, axis=dim_index + 1)
    new_shape = list(padded.shape)
    new_shape[dim_index] = 4 * length
    return stacked.reshape(new_shape)


def refine_both(padded):
    return refine(refine(padded, 1), 2)


def body(controls, members, loc_lon, loc_lat, balance, innovation, obs_weight):
    highest = lax.Precision.HIGHEST
    member_scale = 1.0 / math.sqrt(controls.shape[0] * lax.axis_size("member") - 1)
    full_lon = loc_lon.shape[0]
    stripe_width = full_lon // lax.axis_size("member")
    level_ctrl, level_members = (
        lax.all_to_all(controls, "band", split_axis=1, concat_axis=2, tiled=True),
        lax.all_to_all(members, "band", split_axis=1, concat_axis=2, tiled=True),
    )
    rowwise = jnp.einsum("klyx,ux->klyu", level_ctrl, loc_lon, precision=highest)
    fields = jnp.einsum("vy,klyx->klvx", loc_lat, rowwise, precision=highest)
    partial_value = jnp.sum(level_members * fields, axis=0) * member_scale
    summed = lax.psum(partial_value, "member")
    summed = lax.all_to_all(summed, "band", split_axis=1, concat_axis=0, tiled=True)
    wrapped = jnp.concatenate([summed[:, :, -2:], summed, summed[:, :, :2]], axis=2)
    extended = lax.dynamic_slice_in_dim(
        wrapped, lax.axis_index("member") * stripe_width, stripe_width + 4, 2
    )
    padded = with_halo(extended, (("band", 1),), 2, False)
    fine_field = refine_both(padded)
    grown_field = with_halo(fine_field, (("member", 2),), 1, True)
    grown_field = with_halo(grown_field, (("band", 1),), 1, False)
    balanced = (
        balance[0] * fine_field
        + balance[1] * grown_field[:, 1:-1, 2:]
        + balance[2] * grown_field[:, 1:-1, :-2]
        + balance[3] * grown_field[:, 2:, 1:-1]
        + balance[4] * grown_field[:, :-2, 1:-1]
    )
    weighted_misfit = obs_weight * (balanced - innovation)
    pieces = balance[1:, None] * weighted_misfit[None]
    spread = with_halo(pieces, (("member", 3),), 1, True)
    spread = with_halo(spread, (("band", 2),), 1, False)
    fine_grad = (
        balance[0] * weighted_misfit
        + spread[0][:, 1:-1, :-2]
        + spread[1][:, 1:-1, 2:]
        + spread[2][:, :-2, 1:-1]
        + spread[3][:, 2:, 1:-1]
    )
    unused, pullback = jax.vjp(refine_both, padded)
    coarse_ext = pullback(fine_grad)[0]
    west_rim = passed_along(coarse_ext[:, :, :2], "member", -1)
    east_rim = passed_along(coarse_ext[:, :, -2:], "member", 1)
    core_sum = coarse_ext[:, :, 2:-2]
    core_sum = core_sum.at[:, :, -2:].add(west_rim)
    core_sum = core_sum.at[:, :, :2].add(east_rim)
    south_rim = from_behind(core_sum[:, :2], "band", -1)
    north_rim = from_behind(core_sum[:, -2:], "band", 1)
    coarse_grad = core_sum[:, 2:-2]
    coarse_grad = coarse_grad.at[:, -2:].add(south_rim)
    coarse_grad = coarse_grad.at[:, :2].add(north_rim)
    level_grad = lax.all_to_all(coarse_grad, "band", split_axis=0, concat_axis=1, tiled=True)
    weighted = (
        level_members
        * lax.all_gather(level_grad, "member", axis=2, tiled=True)[None]
        * member_scale
    )
    adjoint = jnp.einsum("klyu,ux->klyx", weighted, loc_lon, precision=highest)
    adjoint = jnp.einsum("vy,klvx->klyx", loc_lat, adjoint, precision=highest)
    adjoint = lax.all_to_all(adjoint, "band", split_axis=2, concat_axis=1, tiled=True)
    return controls + adjoint


def solution(mesh):
    return jax.shard_map(
        body,
        mesh=mesh,
        in_specs=(
            P("member", None, "band", None),
            P("member", None, "band", None),
            P(),
            P(),
            P(None, "band", "member"),
            P(None, "band", "member"),
            P(None, "band", "member"),
        ),
        out_specs=P("member", None, "band", None),
        check_vma=False,
    )
```

profile of v0, /device:TPU:0, one launch (start us, length us, event | category | flops | bytes accessed | tf_op | source)
XLA Modules:
  0.0 769.8 jit_solution(10708017313778358526)
XLA Ops:
  6.5 5.0 copy.99
  11.5 6.3 all-to-all-start
  17.9 4.9 copy.103
  22.8 88.5 %all-to-all-done = f32[2,16,64,512]{3,2,0,1:T(8,128)} async-done(((f32[2,16,64,512]{3,2,0,1:T(8,128)}), f32[2,16,64,512]{3,2,0,1:T(8,128)}, u32[]{:S(2)}, u32[]{:S(2)}) %all-to-all-start) | async-done | bytes 4194336 | tf_op jit(solution)/shard_map/all_to_all | solution.py:73
  111.3 4.9 all-to-all-start.1
  116.2 4.9 copy.101
  121.1 5.3 copy.107
  126.4 82.4 %all-to-all-done.1 = f32[2,16,64,512]{3,2,0,1:T(8,128)} async-done(((f32[2,16,64,512]{3,2,0,1:T(8,128)}), f32[2,16,64,512]{3,2,0,1:T(8,128)}, u32[]{:S(2)}, u32[]{:S(2)}) %all-to-all-start.1) | async-done | bytes 4194336 | tf_op jit(solution)/shard_map/all_to_all | solution.py:72
  208.8 2.8 copy.105
  211.6 7.2 fusion.20
  218.8 4.1 fusion.10
  224.4 61.1 %all-reduce.34.cloned.1.call-done = f32[4,256,512]{1,2,0:T(8,128)} async-done(((f32[4,256,512]{1,2,0:T(8,128)}), f32[4,256,512]{1,2,0:T(8,128)}) %all-reduce.34.cloned.1.call-update) | async-done | bytes 2097168 | tf_op jit(solution)/shard_map/psum | solution.py:78
  285.5 3.1 copy.108
  288.6 4.5 all-to-all-start.2
  293.3 46.9 %all-to-all-done.2 = f32[4,256,512]{2,0,1:T(4,128)S(1)} async-done(((f32[4,256,512]{2,0,1:T(4,128)}), f32[4,256,512]{2,0,1:T(4,128)S(1)}, u32[]{:S(2)}, u32[]{:S(2)}) %all-to-all-start.2) | async-done | bytes 2097184 | tf_op jit(solution)/shard_map/all_to_all | solution.py:79
  344.6 4.2 collective-permute-done.1
  353.4 3.7 pad_maximum_fusion.2
  357.1 8.6 %copy.114 = f32[16,256,64,4]{1,0,3,2:T(8,128)} copy(f32[16,256,64,4]{2,0,1,3:T(8,128)} %pad_maximum_fusion.2) | data formatting | bytes 8388608 | tf_op jit(solution)/shard_map/stack | solution.py:56
  370.5 2.6 pad_maximum_fusion.3
  380.3 5.0 collective-permute-start.5
  390.3 5.5 copy.123
  395.8 5.6 copy.124
  406.6 20.2 %fusion.3 = f32[16,256,256]{1,0,2:T(8,128)} fusion(f32[16,256,256]{1,0,2:T(8,128)} %copy.124, f32[16,256,256]{1,0,2:T(8,128)} %copy.123, f32[16,1,258]{1,0,2:T(8,128)} %copy.122, f32[16,256,1]{1,0,2:T(8,128)S(1)} %collective-permute-done.2, f32[16,256,256]{1,0,2:T(8,128)} %bitcast.240, f32[16,256,1]{1,0,2:T(8,128)S(1)} %collective-permute-done.3, ...), kind=kLoop, calls=%fused_computation.17 | loop fusion | flops 19922944 | bytes 18153728 | tf_op jit(solution)/shard_map/mul | solution.py:95
  426.8 10.8 %broadcast_multiply_fusion = f32[4,16,256,256]{2,1,3,0:T(8,128)} fusion(f32[16,256,256]{1,0,2:T(8,128)} %fusion.3, f32[4,256,256]{1,2,0:T(8,128)} %copy.125), kind=kLoop, calls=%fused_computation.3 | loop fusion | flops 4194304 | bytes 22020096 | tf_op jit(solution)/shard_map/mul | solution.py:96
  438.5 2.6 collective-permute-start.7
  441.1 2.6 collective-permute-done.6
  443.8 6.8 pad_maximum_fusion.1
  450.6 7.3 fusion.39
  457.9 6.5 copy.126
  464.4 3.1 collective-permute-start.8
  467.5 6.5 copy.127
  475.5 6.4 copy.128
  481.9 6.3 copy.129
  488.2 25.8 %pad_maximum_fusion = f32[4,16,258,258]{2,1,3,0:T(8,128)} fusion(f32[4,16,1,258]{2,1,3,0:T(8,128)} %copy.129, f32[4,16,256,1]{2,1,3,0:T(8,128)S(1)} %collective-permute-done.7, f32[4,16,256,256]{2,1,3,0:T(8,128)} %broadcast_multiply_fusion, f32[4,16,256,1]{2,1,3,0:T(8,128)S(1)} %collective-permute-done.6, f32[4,16,1,258]{2,1,3,0:T(8,128)} %copy.128), kind=kLoop, calls=%fused_computation | loop fusion | flops 17040384 | bytes 34080768 | tf_op jit(solution)/shard_map/concatenate | solution.py:20
  514.1 17.6 %slice_bitcast_fusion.3 = (f32[16,258,258]{1,0,2:T(8,128)}, f32[16,258,258]{1,0,2:T(8,128)}, f32[16,258,258]{1,0,2:T(8,128)}, f32[16,258,258]{1,0,2:T(8,128)}) fusion(f32[4,16,258,258]{2,1,3,0:T(8,128)} %pad_maximum_fusion), kind=kLoop, calls=%fused_computation.7 | loop fusion | bytes 34080768 | tf_op jit(solution)/shard_map/squeeze | solution.py:101
  531.7 9.4 %slice_add_fusion = f32[16,256,256]{1,0,2:T(8,128)S(1)} fusion(f32[16,258,258]{1,0,2:T(8,128)} %get-tuple-element.56, f32[16,258,258]{1,0,2:T(8,128)} %get-tuple-element.57, f32[16,258,258]{1,0,2:T(8,128)} %get-tuple-element.58, f32[16,258,258]{1,0,2:T(8,128)} %get-tuple-element.55, f32[16,256,256]{1,0,2:T(8,128)S(1)} %copy-done.1, f32[256,256]{0,1:T(8,128)S(1)} %copy.102), kind=kLoop, calls=%fused_computation.9 | loop fusion | flops 5242880 | bytes 25427968 | tf_op jit(solution)/shard_map/add | solution.py:100
  541.1 3.0 fusion.17
  545.7 5.0 pad_add_fusion
  558.5 15.6 %scatter-add.14 = f32[16,68,64]{2,0,1:T(8,128)S(1)} dynamic-update-slice(f32[16,68,64]{2,0,1:T(8,128)S(1)} %slice.339, f32[16,68,2]{2,0,1:T(8,128)S(1)} %slice_add_fusion.4, s32[]{:T(128)} %constant.132.clone.1, s32[]{:T(128)} %constant.132.clone.1, s32[]{:T(128)} %constant.145.clone.1) | dynamic-update-slice | bytes 17412 | tf_op jit(solution)/shard_map/scatter-add | solution.py:111
  574.8 7.0 scatter-add.15
  583.2 5.2 collective-permute-start.13
  590.4 13.3 %all_to_all.90 = f32[4,1,16384]{2,1,0:T(1,128)S(1)} all-to-all(f32[4,1,16384]{2,1,0:T(1,128)S(1)} %reshape.202), channel_id=1, replica_groups=mesh['member'=8,'band'=4] {'band'}, dimensions={0} | all-to-all | bytes 524288 | tf_op jit(solution)/shard_map/all_to_all | solution.py:118
  607.2 27.2 %all-gather.2.cloned.1.call-done = f32[4,256,512]{1,2,0:T(8,128)} async-done(((f32[4,256,64]{1,2,0:T(8,128)}), f32[4,256,512]{1,2,0:T(8,128)}) %all-gather.2.cloned.1.call-update) | async-done | bytes 2097168 | tf_op jit(solution)/shard_map/all_gather | solution.py:121
  636.3 9.8 %fusion.11 = f32[2,4,256,512]{2,3,1,0:T(8,128)S(1)} fusion(f32[2,4,256,512]{3,2,1,0:T(8,128)} %bitcast.242, f32[4,256,512]{2,1,0:T(8,128)S(1)} %copy.154, f32[512,512]{1,0:T(8,128)S(1)} %copy-done), kind=kOutput, calls=%fused_computation.33 | convolution fusion | flops 6444548096 | bytes 11534336 | tf_op jit(solution)/shard_map/klyu,ux->klyx/dot_general | solution.py:124
  646.1 5.0 convolution_bitcast_fusion
  651.1 5.5 copy.156
  656.5 98.4 %all_to_all.91 = f32[2,4,256,512]{3,1,0,2:T(4,128)S(1)} all-to-all(f32[2,4,256,512]{3,1,0,2:T(4,128)} %copy.156), channel_id=1, replica_groups=mesh['member'=8,'band'=4] {'band'}, dimensions={2} | all-to-all | bytes 8388608 | tf_op jit(solution)/shard_map/all_to_all | solution.py:126
  759.5 3.0 add.233
  (93 shorter events, 58.6 us)
Async XLA Ops:
  6.5 205.0 %copy-start = (f32[512,512]{1,0:T(8,128)S(1)}, f32[512,512]{1,0:T(8,128)}, u32[]{:S(2)}) copy-start(f32[512,512]{1,0:T(8,128)} %param.17) | copy-start | bytes 3145732
  11.5 99.8 %all-to-all-start = ((f32[2,16,64,512]{3,2,0,1:T(8,128)}), f32[2,16,64,512]{3,2,0,1:T(8,128)}, u32[]{:S(2)}, u32[]{:S(2)}) async-start(f32[2,16,64,512]{3,2,0,1:T(8,128)} %copy.99), calls=%async_computation | async-start | bytes 8388608 | tf_op jit(solution)/shard_map/all_to_all | solution.py:73
  111.3 97.5 %all-to-all-start.1 = ((f32[2,16,64,512]{3,2,0,1:T(8,128)}), f32[2,16,64,512]{3,2,0,1:T(8,128)}, u32[]{:S(2)}, u32[]{:S(2)}) async-start(f32[2,16,64,512]{3,2,0,1:T(8,128)} %copy.103), calls=%async_computation.1 | async-start | bytes 8388608 | tf_op jit(solution)/shard_map/all_to_all | solution.py:72
  116.2 169.3 %all-reduce.34.cloned.1.call-start = ((), (), s32[]{:S(2)}) async-start(), calls=%async_computation.5 | async-start | bytes 4194304 | tf_op jit(solution)/shard_map/psum | solution.py:78
  211.5 7.2 copy-start.3
  211.5 7.2 copy-start.4
  288.6 51.6 %all-to-all-start.2 = ((f32[4,256,512]{2,0,1:T(4,128)}), f32[4,256,512]{2,0,1:T(4,128)S(1)}, u32[]{:S(2)}, u32[]{:S(2)}) async-start(f32[4,256,512]{2,0,1:T(4,128)} %copy.108), calls=%async_computation.2 | async-start | bytes 4194304 | tf_op jit(solution)/shard_map/all_to_all | solution.py:79
  293.1 341.3 %all-gather.2.cloned.1.call-start = ((), (), s32[]{:S(2)}) async-start(), calls=%async_computation.6 | async-start | bytes 2359296 | tf_op jit(solution)/shard_map/all_gather | solution.py:121
  341.8 2.7 collective-permute-start
  343.1 5.6 collective-permute-start.1
  366.5 1.4 collective-permute-start.2
  366.5 4.1 collective-permute-start.3
  377.9 24.7 %collective-permute-start.4 = (f32[16,1,258]{2,0,1:T(8,128)S(1)}, f32[16,1,258]{2,0,1:T(8,128)S(1)}, u32[]{:S(2)}, u32[]{:S(2)}) collective-permute-start(f32[16,1,258]{2,0,1:T(8,128)S(1)} %copy.118), channel_id=1, source_target_pairs={{1,0},{2,1},{3,2},{5,4},{6,5},{7,6},{9,8},{10,9},{11,10},{13,12},{... | collective-permute-start | bytes 49544 | tf_op jit(solution)/shard_map/ppermute | solution.py:19
  380.3 23.7 %collective-permute-start.5 = (f32[16,1,258]{2,0,1:T(8,128)S(1)}, f32[16,1,258]{2,0,1:T(8,128)S(1)}, u32[]{:S(2)}, u32[]{:S(2)}) collective-permute-start(f32[16,1,258]{2,0,1:T(8,128)S(1)} %copy.121), channel_id=1, source_target_pairs={{0,1},{1,2},{2,3},{4,5},{5,6},{6,7},{8,9},{9,10},{10,11},{12,13},{... | collective-permute-start | bytes 49544 | tf_op jit(solution)/shard_map/ppermute | solution.py:18
  395.7 5.6 slice-start
  438.4 5.3 collective-permute-start.6
  438.5 5.3 collective-permute-start.7
  464.4 11.1 %collective-permute-start.8 = (f32[4,16,1,258]{3,1,2,0:T(8,128)S(1)}, f32[4,16,1,258]{3,1,2,0:T(8,128)S(1)}, u32[]{:S(2)}, u32[]{:S(2)}) collective-permute-start(f32[4,16,1,258]{3,1,2,0:T(8,128)S(1)} %copy.126), channel_id=1, source_target_pairs={{0,1},{1,2},{2,3},{4,5},{5,6},{6,7},{8,9},{9,10},{10,11},{12,13},{... | collective-permute-start | bytes 198152 | tf_op jit(solution)/shard_map/ppermute | solution.py:18
  474.0 7.9 %collective-permute-start.9 = (f32[4,16,1,258]{3,1,2,0:T(8,128)S(1)}, f32[4,16,1,258]{3,1,2,0:T(8,128)S(1)}, u32[]{:S(2)}, u32[]{:S(2)}) collective-permute-start(f32[4,16,1,258]{3,1,2,0:T(8,128)S(1)} %copy.127), channel_id=1, source_target_pairs={{1,0},{2,1},{3,2},{5,4},{6,5},{7,6},{9,8},{10,9},{11,10},{13,12},{... | collective-permute-start | bytes 198152 | tf_op jit(solution)/shard_map/ppermute | solution.py:19
  514.1 17.6 %copy-start.1 = (f32[16,256,256]{1,0,2:T(8,128)S(1)}, f32[16,256,256]{1,0,2:T(8,128)}, u32[]{:S(2)}) copy-start(f32[16,256,256]{1,0,2:T(8,128)} %fusion.3) | copy-start | bytes 12582916
  554.8 3.1 collective-permute-start.10
  557.0 17.4 %collective-permute-start.11 = (f32[16,68,2]{1,0,2:T(8,128)S(1)}, f32[16,68,2]{1,0,2:T(8,128)S(1)}, u32[]{:S(2)}, u32[]{:S(2)}) collective-permute-start(f32[16,68,2]{1,0,2:T(8,128)S(1)} %copy.149), channel_id=1, source_target_pairs={{0,4},{4,8},{8,12},{12,16},{16,20},{20,24},{24,28},{28,0},{1,5},{5... | collective-permute-start | bytes 26120 | tf_op jit(solution)/shard_map/ppermute | solution.py:26
  581.9 6.5 collective-permute-start.12
  583.2 6.6 collective-permute-start.13
  636.3 9.8 %copy-start.5 = (f32[256,256]{1,0:T(8,128)S(1)}, f32[256,256]{1,0:T(8,128)}, u32[]{:S(2)}) copy-start(f32[256,256]{1,0:T(8,128)} %param.18) | copy-start | bytes 786436
  757.3 2.2 copy-start.2
Sparse Core Ops, SparseCore 0:
  224.5 60.9 all-reduce.33
  607.3 27.0 all-gather.1
where the time goes:
time: 780 us; the launch traced here: 770 us
  waiting for transfers between devices  319 us (41%)
  local copies, waits for them, and re-layouts  158 us (20%)
  blocking collectives  112 us (14%)
  other arithmetic  100 us (13%)
  starting transfers between devices  40.8 us (5%)
  matrix products  25.9 us (3%)
  between operations  14.3 us (2%)
    all_to_all x1, blocking collectives, body(): lax.all_to_all(adjoint, 'band', split_axis=2, concat_axis=1, tiled=True)  98.4 us
    all_to_all x1, waiting for transfers between devices, body(): lax.all_to_all(members, 'band', split_axis=1, concat_axis=2, tiled=True)  88.5 us
    all_to_all x1, waiting for transfers between devices, body(): lax.all_to_all(controls, 'band', split_axis=1, concat_axis=2, tiled=True)  82.4 us
    psum x1, waiting for transfers between devices, body(): summed = lax.psum(partial_value, 'member')  61.1 us
    all_to_all x1, waiting for transfers between devices, body(): lax.all_to_all(summed, 'band', split_axis=1, concat_axis=0, tiled=True)  46.9 us
    concatenate x3, other arithmetic, with_halo(): value = jnp.concatenate([before, value, after], axis=dim)  35.3 us
    all_gather x1, waiting for transfers between devices, body(): lax.all_gather(level_grad, 'member', axis=2, tiled=True)[None]  27.2 us
    unnamed x18, local copies, waits for them, and re-layouts  23.1 us
  transfers between devices with their start and end apart: 19, of which 12 were waited for; matrix products, arithmetic and copies ran while one was open for 8% of the time, Pallas kernels for 0%

commit v1 on v0

--- a/solution.py
+++ b/solution.py
@@ -123,7 +123,10 @@
     )
     adjoint = jnp.einsum("klyu,ux->klyx", weighted, loc_lon, precision=highest)
     adjoint = jnp.einsum("vy,klvx->klyx", loc_lat, adjoint, precision=highest)
-    adjoint = lax.all_to_all(adjoint, "band", split_axis=2, concat_axis=1, tiled=True)
+    adjoint = jnp.concatenate(
+        lax.all_to_all(jnp.stack(jnp.split(adjoint, lax.axis_size("band"), axis=2)), "band", 0, 0),
+        axis=1,
+    )
     return controls + adjoint
 
 

time: 780 us -> 772 us (0.990)
  transfers between devices with their start and end apart: 19 -> 19, of which waited for: 12 -> 12; matrix products, arithmetic and copies ran while one was open for 8% -> 9% of each run, Pallas kernels for 0% -> 0%
where the time goes in v1:
time: 772 us; the launch traced here: 762 us
  waiting for transfers between devices  319 us (41%)
  local copies, waits for them, and re-layouts  151 us (20%)
  blocking collectives  111 us (14%)
  other arithmetic  101 us (13%)
  starting transfers between devices  40.8 us (5%)
  matrix products  25 us (3%)
  between operations  14.3 us (2%)
    all_to_all x1, blocking collectives, body(): lax.all_to_all(jnp.stack(jnp.split(adjoint, lax.axis_size('band'), axis=2...  97.9 us
    all_to_all x1, waiting for transfers between devices, body(): lax.all_to_all(members, 'band', split_axis=1, concat_axis=2, tiled=True)  88.5 us
    all_to_all x1, waiting for transfers between devices, body(): lax.all_to_all(controls, 'band', split_axis=1, concat_axis=2, tiled=True)  82.4 us
    psum x1, waiting for transfers between devices, body(): summed = lax.psum(partial_value, 'member')  61.1 us
    all_to_all x1, waiting for transfers between devices, body(): lax.all_to_all(summed, 'band', split_axis=1, concat_axis=0, tiled=True)  46.9 us
    concatenate x3, other arithmetic, with_halo(): value = jnp.concatenate([before, value, after], axis=dim)  35.3 us
    all_gather x1, waiting for transfers between devices, body(): lax.all_gather(level_grad, 'member', axis=2, tiled=True)[None]  27.2 us
    unnamed x18, local copies, waits for them, and re-layouts  23.1 us
  transfers between devices with their start and end apart: 19, of which 12 were waited for; matrix products, arithmetic and copies ran while one was open for 9% of the time, Pallas kernels for 0%

profile of v1, /device:TPU:0, one launch (start us, length us, event | category | flops | bytes accessed | tf_op | source)
XLA Modules:
  0.0 761.9 jit_solution(12941199593423471205)
XLA Ops:
  6.5 5.0 copy.99
  11.5 6.3 all-to-all-start
  17.9 4.9 copy.103
  22.8 88.5 %all-to-all-done = f32[2,16,64,512]{3,2,0,1:T(8,128)} async-done(((f32[2,16,64,512]{3,2,0,1:T(8,128)}), f32[2,16,64,512]{3,2,0,1:T(8,128)}, u32[]{:S(2)}, u32[]{:S(2)}) %all-to-all-start) | async-done | bytes 4194336 | tf_op jit(solution)/shard_map/all_to_all | solution.py:73
  111.3 4.9 all-to-all-start.1
  116.2 4.9 copy.101
  121.1 5.3 copy.107
  126.4 82.4 %all-to-all-done.1 = f32[2,16,64,512]{3,2,0,1:T(8,128)} async-done(((f32[2,16,64,512]{3,2,0,1:T(8,128)}), f32[2,16,64,512]{3,2,0,1:T(8,128)}, u32[]{:S(2)}, u32[]{:S(2)}) %all-to-all-start.1) | async-done | bytes 4194336 | tf_op jit(solution)/shard_map/all_to_all | solution.py:72
  208.8 2.8 copy.105
  211.6 7.2 fusion.20
  218.8 4.1 fusion.10
  224.4 61.1 %all-reduce.34.cloned.1.call-done = f32[4,256,512]{1,2,0:T(8,128)} async-done(((f32[4,256,512]{1,2,0:T(8,128)}), f32[4,256,512]{1,2,0:T(8,128)}) %all-reduce.34.cloned.1.call-update) | async-done | bytes 2097168 | tf_op jit(solution)/shard_map/psum | solution.py:78
  285.5 3.1 copy.108
  288.6 4.5 all-to-all-start.2
  293.3 46.9 %all-to-all-done.2 = f32[4,256,512]{2,0,1:T(4,128)S(1)} async-done(((f32[4,256,512]{2,0,1:T(4,128)}), f32[4,256,512]{2,0,1:T(4,128)S(1)}, u32[]{:S(2)}, u32[]{:S(2)}) %all-to-all-start.2) | async-done | bytes 2097184 | tf_op jit(solution)/shard_map/all_to_all | solution.py:79
  344.6 4.2 collective-permute-done.1
  353.4 3.7 pad_maximum_fusion.2
  357.1 8.5 %copy.114 = f32[16,256,64,4]{1,0,3,2:T(8,128)} copy(f32[16,256,64,4]{2,0,1,3:T(8,128)} %pad_maximum_fusion.2) | data formatting | bytes 8388608 | tf_op jit(solution)/shard_map/stack | solution.py:56
  367.8 2.6 collective-permute-done.3
  370.5 2.6 pad_maximum_fusion.3
  380.2 5.0 collective-permute-start.5
  390.1 5.5 copy.123
  395.6 5.6 copy.124
  406.5 20.0 %fusion.3 = f32[16,256,256]{1,0,2:T(8,128)} fusion(f32[16,256,256]{1,0,2:T(8,128)} %copy.124, f32[16,256,256]{1,0,2:T(8,128)} %copy.123, f32[16,1,258]{1,0,2:T(8,128)} %copy.122, f32[16,256,1]{1,0,2:T(8,128)S(1)} %collective-permute-done.2, f32[16,256,256]{1,0,2:T(8,128)} %bitcast.247, f32[16,256,1]{1,0,2:T(8,128)S(1)} %collective-permute-done.3, ...), kind=kLoop, calls=%fused_computation.17 | loop fusion | flops 19922944 | bytes 18153728 | tf_op jit(solution)/shard_map/mul | solution.py:95
  426.5 10.8 %broadcast_multiply_fusion = f32[4,16,256,256]{2,1,3,0:T(8,128)} fusion(f32[16,256,256]{1,0,2:T(8,128)} %fusion.3, f32[4,256,256]{1,2,0:T(8,128)} %copy.125), kind=kLoop, calls=%fused_computation.3 | loop fusion | flops 4194304 | bytes 22020096 | tf_op jit(solution)/shard_map/mul | solution.py:96
  438.2 2.6 collective-permute-start.7
  440.8 2.6 collective-permute-done.6
  443.5 6.8 pad_maximum_fusion.1
  450.3 7.3 fusion.39
  457.6 6.5 copy.126
  464.1 3.1 collective-permute-start.8
  467.2 6.5 copy.127
  475.2 6.4 copy.128
  481.6 6.3 copy.129
  487.9 25.8 %pad_maximum_fusion = f32[4,16,258,258]{2,1,3,0:T(8,128)} fusion(f32[4,16,1,258]{2,1,3,0:T(8,128)} %copy.129, f32[4,16,256,1]{2,1,3,0:T(8,128)S(1)} %collective-permute-done.7, f32[4,16,256,256]{2,1,3,0:T(8,128)} %broadcast_multiply_fusion, f32[4,16,256,1]{2,1,3,0:T(8,128)S(1)} %collective-permute-done.6, f32[4,16,1,258]{2,1,3,0:T(8,128)} %copy.128), kind=kLoop, calls=%fused_computation | loop fusion | flops 17040384 | bytes 34080768 | tf_op jit(solution)/shard_map/concatenate | solution.py:20
  513.8 17.6 %slice_bitcast_fusion.3 = (f32[16,258,258]{1,0,2:T(8,128)}, f32[16,258,258]{1,0,2:T(8,128)}, f32[16,258,258]{1,0,2:T(8,128)}, f32[16,258,258]{1,0,2:T(8,128)}) fusion(f32[4,16,258,258]{2,1,3,0:T(8,128)} %pad_maximum_fusion), kind=kLoop, calls=%fused_computation.7 | loop fusion | bytes 34080768 | tf_op jit(solution)/shard_map/squeeze | solution.py:101
  531.4 9.4 %slice_add_fusion = f32[16,256,256]{1,0,2:T(8,128)S(1)} fusion(f32[16,258,258]{1,0,2:T(8,128)} %get-tuple-element.56, f32[16,258,258]{1,0,2:T(8,128)} %get-tuple-element.57, f32[16,258,258]{1,0,2:T(8,128)} %get-tuple-element.58, f32[16,258,258]{1,0,2:T(8,128)} %get-tuple-element.55, f32[16,256,256]{1,0,2:T(8,128)S(1)} %copy-done.1, f32[256,256]{0,1:T(8,128)S(1)} %copy.102), kind=kLoop, calls=%fused_computation.9 | loop fusion | flops 5242880 | bytes 25427968 | tf_op jit(solution)/shard_map/add | solution.py:100
  540.8 3.1 fusion.17
  545.5 5.0 pad_add_fusion
  558.5 15.6 %scatter-add.14 = f32[16,68,64]{2,0,1:T(8,128)S(1)} dynamic-update-slice(f32[16,68,64]{2,0,1:T(8,128)S(1)} %slice.339, f32[16,68,2]{2,0,1:T(8,128)S(1)} %slice_add_fusion.4, s32[]{:T(128)} %constant.132.clone.1, s32[]{:T(128)} %constant.132.clone.1, s32[]{:T(128)} %constant.145.clone.1) | dynamic-update-slice | bytes 17412 | tf_op jit(solution)/shard_map/scatter-add | solution.py:111
  574.8 7.0 scatter-add.15
  583.2 5.2 collective-permute-start.13
  590.3 13.1 %all_to_all.77 = f32[4,1,16384]{2,1,0:T(1,128)S(1)} all-to-all(f32[4,1,16384]{2,1,0:T(1,128)S(1)} %reshape.211), channel_id=1, replica_groups=mesh['member'=8,'band'=4] {'band'}, dimensions={0} | all-to-all | bytes 524288 | tf_op jit(solution)/shard_map/all_to_all | solution.py:118
  606.8 27.2 %all-gather.2.cloned.1.call-done = f32[4,256,512]{1,2,0:T(8,128)} async-done(((f32[4,256,64]{1,2,0:T(8,128)}), f32[4,256,512]{1,2,0:T(8,128)}) %all-gather.2.cloned.1.call-update) | async-done | bytes 2097168 | tf_op jit(solution)/shard_map/all_gather | solution.py:121
  636.2 9.2 %fusion.11 = f32[2,4,256,512]{3,2,1,0:T(8,128)S(1)} fusion(f32[2,4,256,512]{3,2,1,0:T(8,128)} %bitcast.249, f32[4,256,512]{2,1,0:T(8,128)S(1)} %copy.154, f32[512,512]{1,0:T(8,128)S(1)} %copy-done), kind=kOutput, calls=%fused_computation.34 | convolution fusion | flops 6444548096 | bytes 11534336 | tf_op jit(solution)/shard_map/klyu,ux->klyx/dot_general | solution.py:124
  645.4 4.6 convolution_bitcast_fusion
  651.5 97.9 %all_to_all.78 = f32[4,2,4,64,512]{4,3,2,1,0:T(8,128)S(1)} all-to-all(f32[4,2,4,64,512]{4,3,2,1,0:T(8,128)S(1)} %pad_maximum_fusion.12), channel_id=1, replica_groups=mesh['member'=8,'band'=4] {'band'}, dimensions={0} | all-to-all | bytes 8388608 | tf_op jit(solution)/shard_map/all_to_all | solution.py:127
  751.6 3.0 add.233
  (93 shorter events, 55.3 us)
Async XLA Ops:
  6.5 205.0 %copy-start = (f32[512,512]{1,0:T(8,128)S(1)}, f32[512,512]{1,0:T(8,128)}, u32[]{:S(2)}) copy-start(f32[512,512]{1,0:T(8,128)} %param.17) | copy-start | bytes 3145732
  11.5 99.8 %all-to-all-start = ((f32[2,16,64,512]{3,2,0,1:T(8,128)}), f32[2,16,64,512]{3,2,0,1:T(8,128)}, u32[]{:S(2)}, u32[]{:S(2)}) async-start(f32[2,16,64,512]{3,2,0,1:T(8,128)} %copy.99), calls=%async_computation | async-start | bytes 8388608 | tf_op jit(solution)/shard_map/all_to_all | solution.py:73
  111.3 97.5 %all-to-all-start.1 = ((f32[2,16,64,512]{3,2,0,1:T(8,128)}), f32[2,16,64,512]{3,2,0,1:T(8,128)}, u32[]{:S(2)}, u32[]{:S(2)}) async-start(f32[2,16,64,512]{3,2,0,1:T(8,128)} %copy.103), calls=%async_computation.1 | async-start | bytes 8388608 | tf_op jit(solution)/shard_map/all_to_all | solution.py:72
  116.2 169.4 %all-reduce.34.cloned.1.call-start = ((), (), s32[]{:S(2)}) async-start(), calls=%async_computation.5 | async-start | bytes 4194304 | tf_op jit(solution)/shard_map/psum | solution.py:78
  211.6 7.2 copy-start.3
  211.6 7.2 copy-start.4
  288.6 51.6 %all-to-all-start.2 = ((f32[4,256,512]{2,0,1:T(4,128)}), f32[4,256,512]{2,0,1:T(4,128)S(1)}, u32[]{:S(2)}, u32[]{:S(2)}) async-start(f32[4,256,512]{2,0,1:T(4,128)} %copy.108), calls=%async_computation.2 | async-start | bytes 4194304 | tf_op jit(solution)/shard_map/all_to_all | solution.py:79
  293.1 340.9 %all-gather.2.cloned.1.call-start = ((), (), s32[]{:S(2)}) async-start(), calls=%async_computation.6 | async-start | bytes 2359296 | tf_op jit(solution)/shard_map/all_gather | solution.py:121
  341.9 2.7 collective-permute-start
  343.1 5.6 collective-permute-start.1
  366.4 1.4 collective-permute-start.2
  366.4 4.1 collective-permute-start.3
  377.8 24.7 %collective-permute-start.4 = (f32[16,1,258]{2,0,1:T(8,128)S(1)}, f32[16,1,258]{2,0,1:T(8,128)S(1)}, u32[]{:S(2)}, u32[]{:S(2)}) collective-permute-start(f32[16,1,258]{2,0,1:T(8,128)S(1)} %copy.118), channel_id=1, source_target_pairs={{1,0},{2,1},{3,2},{5,4},{6,5},{7,6},{9,8},{10,9},{11,10},{13,12},{... | collective-permute-start | bytes 49544 | tf_op jit(solution)/shard_map/ppermute | solution.py:19
  380.2 23.6 %collective-permute-start.5 = (f32[16,1,258]{2,0,1:T(8,128)S(1)}, f32[16,1,258]{2,0,1:T(8,128)S(1)}, u32[]{:S(2)}, u32[]{:S(2)}) collective-permute-start(f32[16,1,258]{2,0,1:T(8,128)S(1)} %copy.121), channel_id=1, source_target_pairs={{0,1},{1,2},{2,3},{4,5},{5,6},{6,7},{8,9},{9,10},{10,11},{12,13},{... | collective-permute-start | bytes 49544 | tf_op jit(solution)/shard_map/ppermute | solution.py:18
  395.6 5.6 slice-start
  438.1 5.3 collective-permute-start.6
  438.2 5.3 collective-permute-start.7
  464.1 11.1 %collective-permute-start.8 = (f32[4,16,1,258]{3,1,2,0:T(8,128)S(1)}, f32[4,16,1,258]{3,1,2,0:T(8,128)S(1)}, u32[]{:S(2)}, u32[]{:S(2)}) collective-permute-start(f32[4,16,1,258]{3,1,2,0:T(8,128)S(1)} %copy.126), channel_id=1, source_target_pairs={{0,1},{1,2},{2,3},{4,5},{5,6},{6,7},{8,9},{9,10},{10,11},{12,13},{... | collective-permute-start | bytes 198152 | tf_op jit(solution)/shard_map/ppermute | solution.py:18
  473.8 7.9 %collective-permute-start.9 = (f32[4,16,1,258]{3,1,2,0:T(8,128)S(1)}, f32[4,16,1,258]{3,1,2,0:T(8,128)S(1)}, u32[]{:S(2)}, u32[]{:S(2)}) collective-permute-start(f32[4,16,1,258]{3,1,2,0:T(8,128)S(1)} %copy.127), channel_id=1, source_target_pairs={{1,0},{2,1},{3,2},{5,4},{6,5},{7,6},{9,8},{10,9},{11,10},{13,12},{... | collective-permute-start | bytes 198152 | tf_op jit(solution)/shard_map/ppermute | solution.py:19
  513.8 17.6 %copy-start.1 = (f32[16,256,256]{1,0,2:T(8,128)S(1)}, f32[16,256,256]{1,0,2:T(8,128)}, u32[]{:S(2)}) copy-start(f32[16,256,256]{1,0,2:T(8,128)} %fusion.3) | copy-start | bytes 12582916
  554.8 3.1 collective-permute-start.10
  557.0 17.4 %collective-permute-start.11 = (f32[16,68,2]{1,0,2:T(8,128)S(1)}, f32[16,68,2]{1,0,2:T(8,128)S(1)}, u32[]{:S(2)}, u32[]{:S(2)}) collective-permute-start(f32[16,68,2]{1,0,2:T(8,128)S(1)} %copy.149), channel_id=1, source_target_pairs={{0,4},{4,8},{8,12},{12,16},{16,20},{20,24},{24,28},{28,0},{1,5},{5... | collective-permute-start | bytes 26120 | tf_op jit(solution)/shard_map/ppermute | solution.py:26
  581.8 6.5 collective-permute-start.12
  583.2 6.6 collective-permute-start.13
  636.2 9.2 %copy-start.5 = (f32[256,256]{1,0:T(8,128)S(1)}, f32[256,256]{1,0:T(8,128)}, u32[]{:S(2)}) copy-start(f32[256,256]{1,0:T(8,128)} %param.18) | copy-start | bytes 786436
  749.4 2.2 copy-start.2
Sparse Core Ops, SparseCore 0:
  224.5 60.9 all-reduce.33
  607.0 27.0 all-gather.1
